TPU v7x, 256 devices: a whole 4x4x8 slice. The times are simulated.
256 devices in a mesh: dp: 2 (over x_hi), mx: 8 (over z), my: 16 (over x_lo, y, core).
Axes of the slice: x: 4 (x_hi: 2, x_lo: 2; x = x_hi * 2 + x_lo), y: 4, z: 8, core: 2. Of those that a mesh axis runs over, the one named last changes fastest.
Arguments:
- inputs: bfloat16 [2048, 6144], P(('dp', 'my'), 'mx'), may hold values from -6 to 6
- hidden_in: bfloat16 [2048, 24576], P(('dp', 'mx'), 'my'), may hold values from -6 to 6
- out_grad: bfloat16 [2048, 6144], P(('dp', 'my'), 'mx'), may hold values from -6 to 6
- up_weight: bfloat16 [6144, 24576], P('mx', 'my'), may hold values from -0.078125 to 0.078125
- down_weight: bfloat16 [24576, 6144], P('my', 'mx'), may hold values from -0.0390625 to 0.0390625
Outputs:
- inputs_grad: bfloat16 [2048, 6144], P(('dp', 'my'), 'mx')
- up_grad: bfloat16 [6144, 24576], P('mx', 'my')
- down_grad: bfloat16 [24576, 6144], P('my', 'mx')
All inputs are finite; a program needn't handle non-finite values.
Results may differ from a plain program's by a relative error of at most 0.0059.
Values may be sent and summed in bfloat16 or wider, within the bound.
No kernel may reach another device: no remote copies, remote signals or barrier semaphores. Data moves between devices by JAX's collectives and lax.ppermute only.
A program may use at most 64 MiB of HBM per device.

v0:
```python
import jax
import jax.numpy as jnp
from jax import lax
from jax.sharding import PartitionSpec as P


def gelu_value(value):
    return 0.5 * value * (1.0 + lax.erf(value * 0.7071067811865476))


def gelu_slope(value):
    return (
        0.5 * (1.0 + lax.erf(value * 0.7071067811865476))
        + value * jnp.exp(-0.5 * value * value) * 0.3989422804014327
    )


def per_device(inputs, hidden_in, out_grad, up_weight, down_weight):
    total_tokens = out_grad.shape[0] * lax.axis_size("my") * lax.axis_size("dp")
    grad_scale = 1.0 / jnp.sqrt(jnp.float32(total_tokens))
    pre_value = hidden_in.astype(jnp.float32)
    act_local = gelu_value(pre_value).astype(jnp.bfloat16)
    act_whole = lax.all_gather(act_local, "mx", axis=0, tiled=True)
    input_whole, grad_whole = (
        lax.all_gather(inputs, "my", axis=0, tiled=True),
        lax.all_gather(out_grad, "my", axis=0, tiled=True),
    )
    down_part = (
        jnp.einsum("tf,td->fd", act_whole, grad_whole, preferred_element_type=jnp.float32)
        * grad_scale
    )
    row_block = grad_whole
    act_grad = lax.psum_scatter(
        jnp.einsum("td,fd->tf", row_block, down_weight, preferred_element_type=jnp.float32),
        "mx",
        scatter_dimension=0,
        tiled=True,
    )
    pre_grad = (act_grad * gelu_slope(pre_value)).astype(jnp.bfloat16)
    pre_whole = lax.all_gather(pre_grad, "mx", axis=0, tiled=True)
    row_block = pre_whole
    inputs_grad = lax.psum_scatter(
        jnp.einsum("tf,df->td", row_block, up_weight, preferred_element_type=jnp.float32),
        "my",
        scatter_dimension=0,
        tiled=True,
    ).astype(jnp.bfloat16)
    up_part = (
        jnp.einsum("td,tf->df", input_whole, pre_whole, preferred_element_type=jnp.float32)
        * grad_scale
    )
    up_total, down_total = (
        lax.psum(up_part.astype(jnp.bfloat16), "dp").astype(jnp.float32),
        lax.psum(down_part.astype(jnp.bfloat16), "dp").astype(jnp.float32),
    )
    return (inputs_grad, up_total.astype(jnp.bfloat16), down_total.astype(jnp.bfloat16))


def solution(mesh):
    return jax.shard_map(
        per_device,
        mesh=mesh,
        in_specs=(
            P(("dp", "my"), "mx"),
            P(("dp", "mx"), "my"),
            P(("dp", "my"), "mx"),
            P("mx", "my"),
            P("my", "mx"),
        ),
        out_specs=(P(("dp", "my"), "mx"), P("mx", "my"), P("my", "mx")),
        check_vma=False,
    )
```

profile of v0, /device:TPU:4, one launch (start us, length us, event | category | flops | bytes accessed | tf_op | source)
XLA Modules:
  0.0 477.7 jit_solution(6515074767499462279)
XLA Ops:
  7.2 0.0 copy-start
  7.2 0.0 all-gather.5.cloned.1.call-start
  7.2 0.7 all-gather.5.cloned.1.call-update
  7.9 0.0 reduce-scatter.3.cloned.1.call-start
  8.0 40.1 %all-gather.5.cloned.1.call-done = bf16[1024,768]{1,0:T(8,128)(2,1)} async-done(((bf16[64,768]{1,0:T(8,128)(2,1)}), bf16[1024,768]{1,0:T(8,128)(2,1)}) %all-gather.5.cloned.1.call-update) | async-done | bytes 1572880 | tf_op jit(solution)/shard_map/all_gather | solution.py:26
  48.1 0.0 copy-done
  48.1 6.0 %fusion.10 = f32[1024,1536]{1,0:T(8,128)} fusion(bf16[1024,768]{1,0:T(8,128)(2,1)} %all-gather.5.cloned.1.call-done, bf16[1536,768]{1,0:T(8,128)(2,1)S(1)} %copy-done), kind=kOutput, calls=%fused_computation.17 | convolution fusion | flops 2415919104 | bytes 10223616 | tf_op jit(solution)/shard_map/td,fd->tf/dot_general | solution.py:34
  54.0 0.0 copy-start.1
  54.0 0.0 reduce-scatter.3.cloned.1.call-update
  54.1 0.0 all-gather.11.cloned.1.call-start
  54.1 75.5 %reduce-scatter.3.cloned.1.call-done = f32[128,1536]{1,0:T(8,128)} async-done(((f32[1024,1536]{1,0:T(8,128)}), f32[128,1536]{1,0:T(8,128)}) %reduce-scatter.3.cloned.1.call-update) | async-done | bytes 786448 | tf_op jit(solution)/shard_map/reduce_scatter | solution.py:33
  129.6 0.0 copy-done.1
  129.6 2.4 fusion.9
  132.0 0.0 all-gather.11.cloned.1.call-update
  132.0 0.0 all-gather.9.cloned.1.call-start
  132.1 0.5 all-gather.9.cloned.1.call-update
  132.6 0.0 all-gather.7.cloned.1.call-start
  132.7 0.5 all-gather.7.cloned.1.call-update
  133.2 0.0 all-reduce.3.cloned.1.call-start
  133.3 42.5 %all-gather.11.cloned.1.call-done = bf16[1024,1536]{1,0:T(8,128)(2,1)} async-done(((bf16[128,1536]{1,0:T(8,128)(2,1)}), bf16[1024,1536]{1,0:T(8,128)(2,1)}) %all-gather.11.cloned.1.call-update) | async-done | bytes 3145744 | tf_op jit(solution)/shard_map/all_gather | solution.py:23
  175.8 6.4 %multiply_convert_fusion = bf16[1536,768]{1,0:T(8,128)(2,1)} fusion(bf16[1024,1536]{1,0:T(8,128)(2,1)} %all-gather.11.cloned.1.call-done, bf16[1024,768]{1,0:T(8,128)(2,1)} %all-gather.5.cloned.1.call-done), kind=kOutput, calls=%fused_computation | convolution fusion | flops 2418278400 | bytes 7077888 | tf_op jit(solution)/shard_map/tf,td->fd/dot_general | solution.py:29
  182.2 29.2 %all-gather.9.cloned.1.call-done = bf16[1024,768]{1,0:T(8,128)(2,1)} async-done(((bf16[64,768]{1,0:T(8,128)(2,1)}), bf16[1024,768]{1,0:T(8,128)(2,1)}) %all-gather.9.cloned.1.call-update) | async-done | bytes 1572880 | tf_op jit(solution)/shard_map/all_gather | solution.py:25
  211.4 46.9 %all-gather.7.cloned.1.call-done = bf16[1024,1536]{1,0:T(8,128)(2,1)} async-done(((bf16[128,1536]{1,0:T(8,128)(2,1)}), bf16[1024,1536]{1,0:T(8,128)(2,1)}) %all-gather.7.cloned.1.call-update) | async-done | bytes 3145744 | tf_op jit(solution)/shard_map/all_gather | solution.py:40
  258.3 6.4 %fusion = bf16[768,1536]{0,1:T(8,128)(2,1)} fusion(bf16[1024,1536]{1,0:T(8,128)(2,1)} %all-gather.7.cloned.1.call-done, bf16[1024,768]{1,0:T(8,128)(2,1)} %all-gather.9.cloned.1.call-done), kind=kOutput, calls=%fused_computation.2 | convolution fusion | flops 2418278400 | bytes 7077888 | tf_op jit(solution)/shard_map/td,tf->df/dot_general | solution.py:49
  264.8 0.0 all-reduce.3.cloned.1.call-update
  264.8 0.0 reduce-scatter.5.cloned.1.call-start
  264.8 6.9 %fusion.11 = f32[1024,768]{1,0:T(8,128)} fusion(bf16[1024,1536]{1,0:T(8,128)(2,1)} %all-gather.7.cloned.1.call-done, bf16[768,1536]{1,0:T(8,128)(2,1)} %param.8), kind=kOutput, calls=%fused_computation.18 | convolution fusion | flops 2415919104 | bytes 8650752 | tf_op jit(solution)/shard_map/tf,df->td/dot_general | solution.py:43
  271.8 0.0 reduce-scatter.5.cloned.1.call-update
  271.8 121.6 %all-reduce.3.cloned.1.call-done = (bf16[768,1536]{0,1:T(8,128)(2,1)}, bf16[1536,768]{1,0:T(8,128)(2,1)}) async-done(((bf16[768,1536]{0,1:T(8,128)(2,1)}, bf16[1536,768]{1,0:T(8,128)(2,1)}), (bf16[768,1536]{0,1:T(8,128)(2,1)}, bf16[1536,768]{1,0:T(8,128)(2,1)})) %all-reduce.3.cloned.1.call-update) | async-done | bytes 4718608 | tf_op jit(solution)/shard_map/psum | solution.py:53
  393.4 4.3 copy.8
  397.7 68.3 %reduce-scatter.5.cloned.1.call-done = f32[64,768]{1,0:T(8,128)} async-done(((f32[1024,768]{1,0:T(8,128)}), f32[64,768]{1,0:T(8,128)}) %reduce-scatter.5.cloned.1.call-update) | async-done | bytes 196624 | tf_op jit(solution)/shard_map/reduce_scatter | solution.py:42
  466.0 1.6 convert_element_type.27
  467.6 3.2 copy.11
Async XLA Ops:
  7.2 40.9 %copy-start = (bf16[1536,768]{1,0:T(8,128)(2,1)S(1)}, bf16[1536,768]{1,0:T(8,128)(2,1)}, u32[]{:S(2)}) copy-start(bf16[1536,768]{1,0:T(8,128)(2,1)} %param.9) | copy-start | bytes 7077892
  7.2 40.9 %all-gather.5.cloned.1.call-start = ((), (), s32[]{:S(2)}) async-start(), calls=%async_computation.2 | async-start | bytes 1671168 | tf_op jit(solution)/shard_map/all_gather | solution.py:26
  7.9 121.7 %reduce-scatter.3.cloned.1.call-start = ((), (), s32[]{:S(2)}) async-start(), calls=%async_computation.3 | async-start | bytes 7077888 | tf_op jit(solution)/shard_map/reduce_scatter | solution.py:33
  54.0 75.6 %copy-start.1 = (bf16[128,1536]{1,0:T(8,128)(2,1)S(1)}, bf16[128,1536]{1,0:T(8,128)(2,1)}, u32[]{:S(2)}) copy-start(bf16[128,1536]{1,0:T(8,128)(2,1)} %param.6) | copy-start | bytes 1179652
  54.1 121.8 %all-gather.11.cloned.1.call-start = ((), (), s32[]{:S(2)}) async-start(), calls=%async_computation.7 | async-start | bytes 3538944 | tf_op jit(solution)/shard_map/all_gather | solution.py:23
  132.0 79.4 %all-gather.9.cloned.1.call-start = ((), (), s32[]{:S(2)}) async-start(), calls=%async_computation.6 | async-start | bytes 1671168 | tf_op jit(solution)/shard_map/all_gather | solution.py:25
  132.6 125.7 %all-gather.7.cloned.1.call-start = ((), (), s32[]{:S(2)}) async-start(), calls=%async_computation.4 | async-start | bytes 3538944 | tf_op jit(solution)/shard_map/all_gather | solution.py:40
  133.2 260.2 %all-reduce.3.cloned.1.call-start = ((), (), s32[]{:S(2)}) async-start(), calls=%async_computation.8 | async-start | bytes 9437184 | tf_op jit(solution)/shard_map/psum | solution.py:53
  264.8 201.2 %reduce-scatter.5.cloned.1.call-start = ((), (), s32[]{:S(2)}) async-start(), calls=%async_computation.5 | async-start | bytes 3342336 | tf_op jit(solution)/shard_map/reduce_scatter | solution.py:42
Sparse Core Ops, SparseCore 0:
  9.8 38.1 all-gather.4
  54.2 75.3 reduce-scatter.2
  132.2 43.5 all-gather.10
  177.5 33.8 all-gather.8
  213.1 45.2 all-gather.6
  264.9 128.4 all-reduce.2
  396.0 70.0 reduce-scatter.4
where the time goes:
time: 478 us
  waiting for transfers between devices  426 us (89%)
  matrix products  25.8 us (5%)
  between operations  14.1 us (3%)
  local copies, waits for them, and re-layouts  7.51 us (2%)
    psum x1, waiting for transfers between devices, per_device(): lax.psum(up_part.astype(jnp.bfloat16), 'dp').astype(jnp.float32)  122 us
    reduce_scatter x1, waiting for transfers between devices, per_device(): lax.psum_scatter(jnp.einsum('td,fd->tf', row_block, down_weight, preferre...  75.5 us
    reduce_scatter x1, waiting for transfers between devices, per_device(): lax.psum_scatter(jnp.einsum('tf,df->td', row_block, up_weight, preferred_...  68.3 us
    all_gather x1, waiting for transfers between devices, per_device(): pre_whole = lax.all_gather(pre_grad, 'mx', axis=0, tiled=True)  46.9 us
    all_gather x1, waiting for transfers between devices, per_device(): act_whole = lax.all_gather(act_local, 'mx', axis=0, tiled=True)  42.5 us
    all_gather x1, waiting for transfers between devices, per_device(): lax.all_gather(out_grad, 'my', axis=0, tiled=True)  40.1 us
    all_gather x1, waiting for transfers between devices, per_device(): lax.all_gather(inputs, 'my', axis=0, tiled=True)  29.2 us
  transfers between devices with their start and end apart: 7, of which 7 were waited for; matrix products, arithmetic and copies ran while one was open for 4% of the time, Pallas kernels for 0%

commit v1 on v0

--- a/solution.py
+++ b/solution.py
@@ -50,7 +50,7 @@
         * grad_scale
     )
     up_total, down_total = (
-        lax.psum(up_part.astype(jnp.bfloat16), "dp").astype(jnp.float32),
+        jnp.sum(lax.all_gather(up_part.astype(jnp.bfloat16), "dp"), axis=0).astype(jnp.float32),
         lax.psum(down_part.astype(jnp.bfloat16), "dp").astype(jnp.float32),
     )
     return (inputs_grad, up_total.astype(jnp.bfloat16), down_total.astype(jnp.bfloat16))

time: 478 us -> 494 us (1.033)
  other arithmetic: 4.01 us -> 28.9 us
  waiting for transfers between devices: 426 us -> 402 us
  local copies, waits for them, and re-layouts: 7.51 us -> 18.2 us
    all_gather x0 -> x1, waiting for transfers between devices: none -> 61 us  [per_device(): lax.all_gather(up_part.astype(jnp.bfloat16), 'dp')]
    psum x1, waiting for transfers between devices: 122 us -> 79.3 us  [per_device(): lax.psum(down_part.astype(jnp.bfloat16), 'dp').astype(jnp.float32)]
    reduce_scatter x1, waiting for transfers between devices: 68.3 us -> 32.8 us  [per_device(): lax.psum_scatter(jnp.einsum('tf,df->td', row_block, up_weight, preferred_...]
    reduce_sum x0 -> x1, other arithmetic: none -> 24.9 us  [per_device(): jnp.sum(lax.all_gather(up_part.astype(jnp.bfloat16), 'dp'), axis=0)]
    all_gather x0 -> x1, local copies, waits for them, and re-layouts: none -> 10.6 us  [per_device(): lax.all_gather(up_part.astype(jnp.bfloat16), 'dp')]
    all_gather x1, waiting for transfers between devices: 42.5 us -> 32.2 us  [per_device(): act_whole = lax.all_gather(act_local, 'mx', axis=0, tiled=True)]
  transfers between devices with their start and end apart: 7 -> 8, of which waited for: 7 -> 8; matrix products, arithmetic and copies ran while one was open for 4% -> 13% of each run, Pallas kernels for 0% -> 0%
where the time goes in v1:
time: 494 us; the launch traced here: 490 us
  waiting for transfers between devices  402 us (81%)
  other arithmetic  28.9 us (6%)
  matrix products  25.8 us (5%)
  local copies, waits for them, and re-layouts  18.2 us (4%)
  between operations  14.1 us (3%)
    psum x1, waiting for transfers between devices, per_device(): lax.psum(down_part.astype(jnp.bfloat16), 'dp').astype(jnp.float32)  79.3 us
    reduce_scatter x1, waiting for transfers between devices, per_device(): lax.psum_scatter(jnp.einsum('td,fd->tf', row_block, down_weight, preferre...  74.7 us
    all_gather x1, waiting for transfers between devices, per_device(): lax.all_gather(up_part.astype(jnp.bfloat16), 'dp')  61 us
    all_gather x1, waiting for transfers between devices, per_device(): pre_whole = lax.all_gather(pre_grad, 'mx', axis=0, tiled=True)  47.5 us
    all_gather x1, waiting for transfers between devices, per_device(): lax.all_gather(out_grad, 'my', axis=0, tiled=True)  40.1 us
    reduce_scatter x1, waiting for transfers between devices, per_device(): lax.psum_scatter(jnp.einsum('tf,df->td', row_block, up_weight, preferred_...  32.8 us
    all_gather x1, waiting for transfers between devices, per_device(): lax.all_gather(inputs, 'my', axis=0, tiled=True)  32.7 us
    all_gather x1, waiting for transfers between devices, per_device(): act_whole = lax.all_gather(act_local, 'mx', axis=0, tiled=True)  32.2 us
  transfers between devices with their start and end apart: 8, of which 8 were waited for; matrix products, arithmetic and copies ran while one was open for 13% of the time, Pallas kernels for 0%

profile of v1, /device:TPU:4, one launch (start us, length us, event | category | flops | bytes accessed | tf_op | source)
XLA Modules:
  0.0 489.8 jit_solution(16658983185484694640)
XLA Ops:
  7.2 0.0 copy-start
  7.2 0.0 all-gather.7.cloned.1.call-start
  7.2 0.7 all-gather.7.cloned.1.call-update
  7.9 0.0 reduce-scatter.3.cloned.1.call-start
  8.0 40.1 %all-gather.7.cloned.1.call-done = bf16[1024,768]{1,0:T(8,128)(2,1)} async-done(((bf16[64,768]{1,0:T(8,128)(2,1)}), bf16[1024,768]{1,0:T(8,128)(2,1)}) %all-gather.7.cloned.1.call-update) | async-done | bytes 1572880 | tf_op jit(solution)/shard_map/all_gather | solution.py:26
  48.1 0.0 copy-done
  48.1 6.1 %fusion.10 = f32[1024,1536]{1,0:T(8,128)} fusion(bf16[1024,768]{1,0:T(8,128)(2,1)} %all-gather.7.cloned.1.call-done, bf16[1536,768]{1,0:T(8,128)(2,1)S(1)} %copy-done), kind=kOutput, calls=%fused_computation.17 | convolution fusion | flops 2415919104 | bytes 10223616 | tf_op jit(solution)/shard_map/td,fd->tf/dot_general | solution.py:34
  54.1 0.0 copy-start.1
  54.2 0.0 reduce-scatter.3.cloned.1.call-update
  54.2 0.0 all-gather.11.cloned.1.call-start
  54.2 0.7 all-gather.11.cloned.1.call-update
  54.9 0.0 all-gather.9.cloned.1.call-start
  55.0 74.7 %reduce-scatter.3.cloned.1.call-done = f32[128,1536]{1,0:T(8,128)} async-done(((f32[1024,1536]{1,0:T(8,128)}), f32[128,1536]{1,0:T(8,128)}) %reduce-scatter.3.cloned.1.call-update) | async-done | bytes 786448 | tf_op jit(solution)/shard_map/reduce_scatter | solution.py:33
  129.7 0.0 copy-done.1
  129.7 2.4 fusion.9
  132.1 0.0 all-gather.9.cloned.1.call-update
  132.1 0.0 all-gather.13.cloned.1.call-start
  132.2 0.5 all-gather.13.cloned.1.call-update
  132.7 0.0 all-gather.15.cloned.1.call-start
  132.8 32.7 %all-gather.11.cloned.1.call-done = bf16[1024,768]{1,0:T(8,128)(2,1)} async-done(((bf16[64,768]{1,0:T(8,128)(2,1)}), bf16[1024,768]{1,0:T(8,128)(2,1)}) %all-gather.11.cloned.1.call-update) | async-done | bytes 1572880 | tf_op jit(solution)/shard_map/all_gather | solution.py:25
  165.5 47.5 %all-gather.9.cloned.1.call-done = bf16[1024,1536]{1,0:T(8,128)(2,1)} async-done(((bf16[128,1536]{1,0:T(8,128)(2,1)}), bf16[1024,1536]{1,0:T(8,128)(2,1)}) %all-gather.9.cloned.1.call-update) | async-done | bytes 3145744 | tf_op jit(solution)/shard_map/all_gather | solution.py:40
  212.9 6.4 %fusion = bf16[768,1536]{0,1:T(8,128)(2,1)} fusion(bf16[1024,1536]{1,0:T(8,128)(2,1)} %all-gather.9.cloned.1.call-done, bf16[1024,768]{1,0:T(8,128)(2,1)} %all-gather.11.cloned.1.call-done), kind=kOutput, calls=%fused_computation.2 | convolution fusion | flops 2418278400 | bytes 7077888 | tf_op jit(solution)/shard_map/td,tf->df/dot_general | solution.py:49
  219.4 0.0 all-gather.15.cloned.1.call-update
  219.4 0.0 reduce-scatter.5.cloned.1.call-start
  219.5 6.9 %fusion.11 = f32[1024,768]{1,0:T(8,128)} fusion(bf16[1024,1536]{1,0:T(8,128)(2,1)} %all-gather.9.cloned.1.call-done, bf16[768,1536]{1,0:T(8,128)(2,1)} %param.8), kind=kOutput, calls=%fused_computation.18 | convolution fusion | flops 2415919104 | bytes 8650752 | tf_op jit(solution)/shard_map/tf,df->td/dot_general | solution.py:43
  226.4 0.0 reduce-scatter.5.cloned.1.call-update
  226.4 0.2 all-reduce.2.cloned.1.call-start
  226.6 32.2 %all-gather.13.cloned.1.call-done = bf16[1024,1536]{1,0:T(8,128)(2,1)} async-done(((bf16[128,1536]{1,0:T(8,128)(2,1)}), bf16[1024,1536]{1,0:T(8,128)(2,1)}) %all-gather.13.cloned.1.call-update) | async-done | bytes 3145744 | tf_op jit(solution)/shard_map/all_gather | solution.py:23
  258.8 6.4 %multiply_convert_fusion = bf16[1536,768]{1,0:T(8,128)(2,1)} fusion(bf16[1024,1536]{1,0:T(8,128)(2,1)} %all-gather.13.cloned.1.call-done, bf16[1024,768]{1,0:T(8,128)(2,1)} %all-gather.7.cloned.1.call-done), kind=kOutput, calls=%fused_computation | convolution fusion | flops 2418278400 | bytes 7077888 | tf_op jit(solution)/shard_map/tf,td->fd/dot_general | solution.py:29
  265.2 0.0 all-reduce.2.cloned.1.call-update
  265.2 61.0 %all-gather.15.cloned.1.call-done = bf16[1536,1536]{0,1:T(8,128)(2,1)} async-done(((bf16[768,1536]{0,1:T(8,128)(2,1)}), bf16[1536,1536]{0,1:T(8,128)(2,1)}) %all-gather.15.cloned.1.call-update) | async-done | bytes 4718608 | tf_op jit(solution)/shard_map/all_gather | solution.py:53
  326.2 10.6 %reshape.6 = bf16[2,768,1536]{1,0,2:T(2,128)(2,1)} reshape(bf16[1536,1536]{0,1:T(8,128)(2,1)} %all-gather.15.cloned.1.call-done) | data formatting | bytes 9437184 | tf_op jit(solution)/shard_map/all_gather | solution.py:53
  336.9 24.9 %reduce_sum.12 = bf16[768,1536]{0,1:T(8,128)(2,1)} reduce(bf16[2,768,1536]{1,0,2:T(2,128)(2,1)} %reshape.6, bf16[]{:T(256)} %constant.6.clone.1), dimensions={0}, to_apply=%region_2.0 | reduce | flops 1179648 | bytes 7077890 | tf_op jit(solution)/shard_map/reduce_sum | solution.py:53
  361.8 4.3 copy.8
  366.1 32.8 %reduce-scatter.5.cloned.1.call-done = f32[64,768]{1,0:T(8,128)} async-done(((f32[1024,768]{1,0:T(8,128)}), f32[64,768]{1,0:T(8,128)}) %reduce-scatter.5.cloned.1.call-update) | async-done | bytes 196624 | tf_op jit(solution)/shard_map/reduce_scatter | solution.py:42
  398.9 1.6 convert_element_type.29
  400.4 79.3 %all-reduce.2.cloned.1.call-done = bf16[1536,768]{1,0:T(8,128)(2,1)} async-done(((bf16[1536,768]{1,0:T(8,128)(2,1)}), bf16[1536,768]{1,0:T(8,128)(2,1)}) %all-reduce.2.cloned.1.call-update) | async-done | bytes 2359312 | tf_op jit(solution)/shard_map/psum | solution.py:54
  479.8 3.2 copy.10
Async XLA Ops:
  7.2 40.9 %copy-start = (bf16[1536,768]{1,0:T(8,128)(2,1)S(1)}, bf16[1536,768]{1,0:T(8,128)(2,1)}, u32[]{:S(2)}) copy-start(bf16[1536,768]{1,0:T(8,128)(2,1)} %param.9) | copy-start | bytes 7077892
  7.2 40.9 %all-gather.7.cloned.1.call-start = ((), (), s32[]{:S(2)}) async-start(), calls=%async_computation.2 | async-start | bytes 1671168 | tf_op jit(solution)/shard_map/all_gather | solution.py:26
  7.9 121.8 %reduce-scatter.3.cloned.1.call-start = ((), (), s32[]{:S(2)}) async-start(), calls=%async_computation.3 | async-start | bytes 7077888 | tf_op jit(solution)/shard_map/reduce_scatter | solution.py:33
  54.1 75.5 %copy-start.1 = (bf16[128,1536]{1,0:T(8,128)(2,1)S(1)}, bf16[128,1536]{1,0:T(8,128)(2,1)}, u32[]{:S(2)}) copy-start(bf16[128,1536]{1,0:T(8,128)(2,1)} %param.6) | copy-start | bytes 1179652
  54.2 111.3 %all-gather.11.cloned.1.call-start = ((), (), s32[]{:S(2)}) async-start(), calls=%async_computation.6 | async-start | bytes 1671168 | tf_op jit(solution)/shard_map/all_gather | solution.py:25
  54.9 158.0 %all-gather.9.cloned.1.call-start = ((), (), s32[]{:S(2)}) async-start(), calls=%async_computation.4 | async-start | bytes 3538944 | tf_op jit(solution)/shard_map/all_gather | solution.py:40
  132.1 126.7 %all-gather.13.cloned.1.call-start = ((), (), s32[]{:S(2)}) async-start(), calls=%async_computation.7 | async-start | bytes 3538944 | tf_op jit(solution)/shard_map/all_gather | solution.py:23
  132.7 193.5 %all-gather.15.cloned.1.call-start = ((), (), s32[]{:S(2)}) async-start(), calls=%async_computation.9 | async-start | bytes 7077888 | tf_op jit(solution)/shard_map/all_gather | solution.py:53
  219.4 179.5 %reduce-scatter.5.cloned.1.call-start = ((), (), s32[]{:S(2)}) async-start(), calls=%async_computation.5 | async-start | bytes 3342336 | tf_op jit(solution)/shard_map/reduce_scatter | solution.py:42
  226.4 253.4 %all-reduce.2.cloned.1.call-start = ((), (), s32[]{:S(2)}) async-start(), calls=%async_computation.8 | async-start | bytes 4718592 | tf_op jit(solution)/shard_map/psum | solution.py:54
Sparse Core Ops, SparseCore 0:
  9.8 38.1 all-gather.6
  54.3 75.3 reduce-scatter.2
  131.5 33.8 all-gather.10
  167.7 45.2 all-gather.8
  215.2 43.5 all-gather.12
  261.0 65.1 all-gather.14
  328.8 70.0 reduce-scatter.4
  401.5 78.2 all-reduce.1
